TPU v7x, 256 devices: a whole 4x4x8 slice. The times are simulated.
256 devices in a mesh: dp: 32 (over z_hi, y, core), expert: 8 (over x, z_lo).
Axes of the slice: x: 4, y: 4, z: 8 (z_hi: 4, z_lo: 2; z = z_hi * 2 + z_lo), core: 2. Of those that a mesh axis runs over, the one named last changes fastest.
Arguments:
- tokens: bfloat16 [49152, 2048], P(('dp', 'expert')), may hold values from -24 to 24
- routes: int32 [49152, 6], P(('dp', 'expert')), may hold values from 0 to 63, as said below
- gate_scale: float32 [49152, 6], P(('dp', 'expert')), may hold values from 0.2 to 2
- w_gate: bfloat16 [8, 2048, 768], P('expert', 'dp'), may hold values from -0.125 to 0.125
- w_up: bfloat16 [8, 2048, 768], P('expert', 'dp'), may hold values from -0.125 to 0.125
- w_down: bfloat16 [8, 2048, 768], P('expert', 'dp'), may hold values from -0.21875 to 0.21875
- d_out: bfloat16 [49152, 2048], P(('dp', 'expert')), may hold values from -24 to 24
Outputs:
- layer_out: bfloat16 [49152, 2048], P(('dp', 'expert'))
- d_tokens: bfloat16 [49152, 2048], P(('dp', 'expert'))
- grad_gate: float32 [8, 2048, 768], P('expert', 'dp')
- grad_up: float32 [8, 2048, 768], P('expert', 'dp')
- grad_down: float32 [8, 2048, 768], P('expert', 'dp')
Inputs may be any that keep to these rules, and one draw needn't show every extreme that they name: `routes`: each token names 6 different experts. The experts of this window are 0 to 7; among the 192 tokens of one device no window expert is named by more than 32 tokens.
All inputs are finite; a program needn't handle non-finite values.
Results may differ from a plain program's by a relative error of at most 0.02.
Values may be sent and summed in bfloat16 or wider, within the bound.
A program may use at most 64 MiB of HBM per device.

v0:
```python
import jax
import jax.numpy as jnp
from jax import lax
from jax.sharding import PartitionSpec as P

CAP = 32


def shards(tokens, routes, gate_scale, w_gate, w_up, w_down, d_out):
    experts_here = lax.axis_size("expert")
    tok_count = tokens.shape[0]
    width = tokens.shape[1]
    choices_per = routes.shape[1]
    capacity = CAP
    slots = experts_here * capacity
    flat_count = tok_count * choices_per
    combine = gate_scale / jnp.sum(gate_scale, axis=1, keepdims=True)
    flat_ids = routes.reshape(flat_count)
    flat_weight = combine.reshape(flat_count)
    live = flat_ids < experts_here
    onehot = (
        (flat_ids[:, None] == jnp.arange(experts_here, dtype=jnp.int32)[None, :]) & live[:, None]
    ).astype(jnp.int32)
    position = jnp.sum((jnp.cumsum(onehot, axis=0) - onehot) * onehot, axis=1)
    dest = jnp.where(live, flat_ids * capacity + position, slots)
    match = jnp.arange(slots, dtype=jnp.int32)[:, None] == dest[None, :]
    filled = jnp.any(match, axis=1)
    owner = jnp.sum(
        jnp.where(match, (jnp.arange(flat_count, dtype=jnp.int32) // choices_per)[None, :], 0),
        axis=1,
    )
    slot_weight = jnp.sum(jnp.where(match, flat_weight[None, :], 0.0), axis=1)
    send_x = jnp.where(filled[:, None], tokens[owner], jnp.zeros((), jnp.bfloat16))
    send_d = jnp.where(
        filled[:, None], d_out[owner].astype(jnp.float32) * slot_weight[:, None], 0.0
    ).astype(jnp.bfloat16)
    send_x = send_x.reshape(experts_here, capacity, width)
    send_d = send_d.reshape(experts_here, capacity, width)
    full_gate, full_up, full_down = (
        lax.all_gather(w_gate, "dp", axis=1, tiled=True),
        lax.all_gather(w_up, "dp", axis=1, tiled=True),
        lax.all_gather(w_down, "dp", axis=1, tiled=True),
    )
    recv_x, recv_d = (
        lax.all_to_all(send_x, "expert", split_axis=0, concat_axis=0, tiled=True),
        lax.all_to_all(send_d, "expert", split_axis=0, concat_axis=0, tiled=True),
    )
    weight_gate = full_gate[0]
    weight_up = full_up[0]
    weight_down = full_down[0]
    rows_x = recv_x.reshape(slots, width)
    rows_d = recv_d.reshape(slots, width)
    contract_last = (((1,), (1,)), ((), ()))
    contract_first = (((0,), (0,)), ((), ()))
    gate = jnp.dot(rows_x, weight_gate, preferred_element_type=jnp.float32)
    up = jnp.dot(rows_x, weight_up, preferred_element_type=jnp.float32)
    sig = jax.nn.sigmoid(gate)
    act = gate * sig
    hidden = (act * up).astype(jnp.bfloat16)
    expert_out = lax.dot_general(
        hidden, weight_down, contract_last, preferred_element_type=jnp.float32
    ).astype(jnp.bfloat16)
    d_hidden = jnp.dot(rows_d, weight_down, preferred_element_type=jnp.float32)
    d_gate = (d_hidden * up * sig * (1.0 + gate * (1.0 - sig))).astype(jnp.bfloat16)
    d_up = (d_hidden * act).astype(jnp.bfloat16)
    d_in = (
        lax.dot_general(d_gate, weight_gate, contract_last, preferred_element_type=jnp.float32)
        + lax.dot_general(d_up, weight_up, contract_last, preferred_element_type=jnp.float32)
    ).astype(jnp.bfloat16)
    back_out, back_in = (
        lax.all_to_all(
            expert_out.reshape(experts_here, capacity, width),
            "expert",
            split_axis=0,
            concat_axis=0,
            tiled=True,
        ),
        lax.all_to_all(
            d_in.reshape(experts_here, capacity, width),
            "expert",
            split_axis=0,
            concat_axis=0,
            tiled=True,
        ),
    )
    term_gate = lax.dot_general(rows_x, d_gate, contract_first, preferred_element_type=jnp.float32)
    term_up = lax.dot_general(rows_x, d_up, contract_first, preferred_element_type=jnp.float32)
    term_down = lax.dot_general(rows_d, hidden, contract_first, preferred_element_type=jnp.float32)
    grad_gate, grad_up, grad_down = (
        lax.psum_scatter(
            term_gate.astype(jnp.bfloat16), "dp", scatter_dimension=0, tiled=True
        ).astype(jnp.float32),
        lax.psum_scatter(
            term_up.astype(jnp.bfloat16), "dp", scatter_dimension=0, tiled=True
        ).astype(jnp.float32),
        lax.psum_scatter(
            term_down.astype(jnp.bfloat16), "dp", scatter_dimension=0, tiled=True
        ).astype(jnp.float32),
    )
    back_out = back_out.reshape(slots, width)
    back_in = back_in.reshape(slots, width)
    dest_tok = dest.reshape(tok_count, choices_per)
    live_tok = live.reshape(tok_count, choices_per)
    weight_tok = jnp.where(live_tok, combine, 0.0)
    safe_rows = jnp.where(live_tok, dest_tok, 0)
    total_out = jnp.zeros((tok_count, width), jnp.float32)
    total_in = jnp.zeros((tok_count, width), jnp.float32)
    for choice_index in range(choices_per):
        rows_pick = safe_rows[:, choice_index]
        total_out = total_out + weight_tok[:, choice_index : choice_index + 1] * back_out[
            rows_pick
        ].astype(jnp.float32)
        total_in = total_in + jnp.where(
            live_tok[:, choice_index : choice_index + 1],
            back_in[rows_pick].astype(jnp.float32),
            0.0,
        )
    layer_out = total_out.astype(jnp.bfloat16)
    d_tokens = total_in.astype(jnp.bfloat16)
    return (layer_out, d_tokens, grad_gate[None], grad_up[None], grad_down[None])


def solution(mesh):
    placed = (
        P(("dp", "expert"), None),
        P(("dp", "expert"), None),
        P(("dp", "expert"), None),
        P("expert", "dp", None),
        P("expert", "dp", None),
        P("expert", "dp", None),
        P(("dp", "expert"), None),
    )
    return jax.shard_map(
        shards,
        mesh=mesh,
        in_specs=placed,
        out_specs=(
            P(("dp", "expert"), None),
            P(("dp", "expert"), None),
            P("expert", "dp", None),
            P("expert", "dp", None),
            P("expert", "dp", None),
        ),
        check_vma=False,
    )
```

profile of v0, /device:TPU:2, one launch (start us, length us, event | category | flops | bytes accessed | tf_op | source)
XLA Modules:
  0.0 494.1 jit_solution(7565816909941220168)
XLA Ops:
  18.6 6.3 %all-to-all-start.2 = ((bf16[8,32,2048]{2,1,0:T(8,128)(2,1)}), bf16[8,32,2048]{2,1,0:T(8,128)(2,1)S(1)}, u32[]{:S(2)}, u32[]{:S(2)}) async-start(bf16[8,32,2048]{2,1,0:T(8,128)(2,1)} %fusion.22), calls=%async_computation.2 | async-start | bytes 2097152 | tf_op jit(solution)/shard_map/all_to_all | solution.py:46
  25.0 2.3 gather_fusion
  27.3 2.4 broadcast_select_fusion
  29.7 11.4 %all-to-all-done.2 = bf16[8,32,2048]{2,1,0:T(8,128)(2,1)S(1)} async-done(((bf16[8,32,2048]{2,1,0:T(8,128)(2,1)}), bf16[8,32,2048]{2,1,0:T(8,128)(2,1)S(1)}, u32[]{:S(2)}, u32[]{:S(2)}) %all-to-all-start.2) | async-done | bytes 1048608 | tf_op jit(solution)/shard_map/all_to_all | solution.py:46
  42.1 6.1 %all-to-all-start = ((bf16[8,32,2048]{2,1,0:T(8,128)(2,1)}), bf16[8,32,2048]{2,1,0:T(8,128)(2,1)S(1)}, u32[]{:S(2)}, u32[]{:S(2)}) async-start(bf16[8,32,2048]{2,1,0:T(8,128)(2,1)} %broadcast_select_fusion), calls=%async_computation | async-start | bytes 2097152 | tf_op jit(solution)/shard_map/all_to_all | solution.py:45
  48.3 27.3 %all-gather.8.cloned.1.call-done = bf16[1,2048,768]{2,1,0:T(8,128)(2,1)} async-done(((bf16[1,64,768]{2,1,0:T(8,128)(2,1)}), bf16[1,2048,768]{2,1,0:T(8,128)(2,1)}) %all-gather.8.cloned.1.call-update) | async-done | bytes 3145744 | tf_op jit(solution)/shard_map/all_gather | solution.py:42
  75.6 4.1 fusion
  79.6 52.9 %all-gather.6.cloned.1.call-done = bf16[1,2048,768]{2,1,0:T(8,128)(2,1)} async-done(((bf16[1,64,768]{2,1,0:T(8,128)(2,1)}), bf16[1,2048,768]{2,1,0:T(8,128)(2,1)}) %all-gather.6.cloned.1.call-update) | async-done | bytes 3145744 | tf_op jit(solution)/shard_map/all_gather | solution.py:41
  132.5 3.7 fusion.6
  136.2 53.7 %all-gather.4.cloned.1.call-done = bf16[1,2048,768]{2,1,0:T(8,128)(2,1)} async-done(((bf16[1,64,768]{2,1,0:T(8,128)(2,1)}), bf16[1,2048,768]{2,1,0:T(8,128)(2,1)}) %all-gather.4.cloned.1.call-update) | async-done | bytes 3145744 | tf_op jit(solution)/shard_map/all_gather | solution.py:40
  189.9 4.3 multiply_convert_fusion.1
  194.9 2.8 convolution_convert_fusion
  197.8 2.7 convolution_convert_fusion.2
  201.5 3.0 fusion.4
  206.6 5.3 %all-to-all-start.3 = ((bf16[8,32,2048]{2,1,0:T(8,128)(2,1)}), bf16[8,32,2048]{2,1,0:T(8,128)(2,1)S(1)}, u32[]{:S(2)}, u32[]{:S(2)}) async-start(bf16[8,32,2048]{2,1,0:T(8,128)(2,1)} %bitcast.104), calls=%async_computation.3 | async-start | bytes 2097152 | tf_op jit(solution)/shard_map/all_to_all | solution.py:78
  212.0 2.7 convolution_convert_fusion.1
  215.7 3.9 fusion.18
  219.6 6.4 %all-to-all-done.3 = bf16[8,32,2048]{2,1,0:T(8,128)(2,1)S(1)} async-done(((bf16[8,32,2048]{2,1,0:T(8,128)(2,1)}), bf16[8,32,2048]{2,1,0:T(8,128)(2,1)S(1)}, u32[]{:S(2)}, u32[]{:S(2)}) %all-to-all-start.3) | async-done | bytes 1048608 | tf_op jit(solution)/shard_map/all_to_all | solution.py:78
  226.0 5.6 %all-to-all-start.1 = ((bf16[8,32,2048]{2,1,0:T(8,128)(2,1)}), bf16[8,32,2048]{2,1,0:T(8,128)(2,1)S(1)}, u32[]{:S(2)}, u32[]{:S(2)}) async-start(bf16[8,32,2048]{2,1,0:T(8,128)(2,1)} %bitcast.107), calls=%async_computation.1 | async-start | bytes 2097152 | tf_op jit(solution)/shard_map/all_to_all | solution.py:71
  234.0 10.8 %all-to-all-done.1 = bf16[8,32,2048]{2,1,0:T(8,128)(2,1)S(1)} async-done(((bf16[8,32,2048]{2,1,0:T(8,128)(2,1)}), bf16[8,32,2048]{2,1,0:T(8,128)(2,1)S(1)}, u32[]{:S(2)}, u32[]{:S(2)}) %all-to-all-start.1) | async-done | bytes 1048608 | tf_op jit(solution)/shard_map/all_to_all | solution.py:71
  267.3 4.1 add_convert_fusion
  273.3 18.0 %reduce-scatter.8.cloned.1.call-done = bf16[64,768]{1,0:T(8,128)(2,1)} async-done(((bf16[2048,768]{1,0:T(8,128)(2,1)}), bf16[64,768]{1,0:T(8,128)(2,1)}) %reduce-scatter.8.cloned.1.call-update) | async-done | bytes 98320 | tf_op jit(solution)/shard_map/reduce_scatter | solution.py:96
  292.9 95.8 %reduce-scatter.4.cloned.1.call-done = bf16[64,768]{1,0:T(8,128)(2,1)} async-done(((bf16[2048,768]{1,0:T(8,128)(2,1)}), bf16[64,768]{1,0:T(8,128)(2,1)}) %reduce-scatter.4.cloned.1.call-update) | async-done | bytes 98320 | tf_op jit(solution)/shard_map/reduce_scatter | solution.py:90
  390.3 95.4 %reduce-scatter.6.cloned.1.call-done = bf16[64,768]{1,0:T(8,128)(2,1)} async-done(((bf16[2048,768]{1,0:T(8,128)(2,1)}), bf16[64,768]{1,0:T(8,128)(2,1)}) %reduce-scatter.6.cloned.1.call-update) | async-done | bytes 98320 | tf_op jit(solution)/shard_map/reduce_scatter | solution.py:93
  (101 shorter events, 48.6 us)
Async XLA Ops:
  7.2 8.8 %copy-start = (bf16[192,2048]{1,0:T(8,128)(2,1)S(1)}, bf16[192,2048]{1,0:T(8,128)(2,1)}, u32[]{:S(2)}) copy-start(bf16[192,2048]{1,0:T(8,128)(2,1)} %param.13) | copy-start | bytes 2359300
  7.2 68.4 %all-gather.8.cloned.1.call-start = ((), (), s32[]{:S(2)}) async-start(), calls=%async_computation.9 | async-start | bytes 3244032 | tf_op jit(solution)/shard_map/all_gather | solution.py:42
  7.9 124.6 %all-gather.6.cloned.1.call-start = ((), (), s32[]{:S(2)}) async-start(), calls=%async_computation.8 | async-start | bytes 3244032 | tf_op jit(solution)/shard_map/all_gather | solution.py:41
  8.7 181.2 %all-gather.4.cloned.1.call-start = ((), (), s32[]{:S(2)}) async-start(), calls=%async_computation.7 | async-start | bytes 3244032 | tf_op jit(solution)/shard_map/all_gather | solution.py:40
  18.6 6.3 %copy-start.1 = (bf16[192,2048]{1,0:T(8,128)(2,1)S(1)}, bf16[192,2048]{1,0:T(8,128)(2,1)}, u32[]{:S(2)}) copy-start(bf16[192,2048]{1,0:T(8,128)(2,1)} %param.7) | copy-start | bytes 2359300
  18.6 22.5 %all-to-all-start.2 = ((bf16[8,32,2048]{2,1,0:T(8,128)(2,1)}), bf16[8,32,2048]{2,1,0:T(8,128)(2,1)S(1)}, u32[]{:S(2)}, u32[]{:S(2)}) async-start(bf16[8,32,2048]{2,1,0:T(8,128)(2,1)} %fusion.22), calls=%async_computation.2 | async-start | bytes 2097152 | tf_op jit(solution)/shard_map/all_to_all | solution.py:46
  42.1 37.5 %all-to-all-start = ((bf16[8,32,2048]{2,1,0:T(8,128)(2,1)}), bf16[8,32,2048]{2,1,0:T(8,128)(2,1)S(1)}, u32[]{:S(2)}, u32[]{:S(2)}) async-start(bf16[8,32,2048]{2,1,0:T(8,128)(2,1)} %broadcast_select_fusion), calls=%async_computation | async-start | bytes 2097152 | tf_op jit(solution)/shard_map/all_to_all | solution.py:45
  48.3 243.1 %reduce-scatter.8.cloned.1.call-start = ((), (), s32[]{:S(2)}) async-start(), calls=%async_computation.12 | async-start | bytes 3244032 | tf_op jit(solution)/shard_map/reduce_scatter | solution.py:96
  136.2 58.7 %copy-start.3 = (bf16[8,32,2048]{2,1,0:T(8,128)(2,1)S(1)}, bf16[8,32,2048]{2,1,0:T(8,128)(2,1)}, u32[]{:S(2)}) copy-start(bf16[8,32,2048]{2,1,0:T(8,128)(2,1)} %copy-done.2) | copy-start | bytes 3145732
  197.7 191.0 %reduce-scatter.4.cloned.1.call-start = ((), (), s32[]{:S(2)}) async-start(), calls=%async_computation.10 | async-start | bytes 3244032 | tf_op jit(solution)/shard_map/reduce_scatter | solution.py:90
  201.5 3.1 copy-start.4
  206.6 5.3 %copy-start.13 = (bf16[256,768]{1,0:T(8,128)(2,1)S(1)}, bf16[256,768]{1,0:T(8,128)(2,1)}, u32[]{:S(2)}) copy-start(bf16[256,768]{1,0:T(8,128)(2,1)} %get-tuple-element.15) | copy-start | bytes 1179652
  206.6 19.4 %all-to-all-start.3 = ((bf16[8,32,2048]{2,1,0:T(8,128)(2,1)}), bf16[8,32,2048]{2,1,0:T(8,128)(2,1)S(1)}, u32[]{:S(2)}, u32[]{:S(2)}) async-start(bf16[8,32,2048]{2,1,0:T(8,128)(2,1)} %bitcast.104), calls=%async_computation.3 | async-start | bytes 2097152 | tf_op jit(solution)/shard_map/all_to_all | solution.py:78
  212.0 273.7 %reduce-scatter.6.cloned.1.call-start = ((), (), s32[]{:S(2)}) async-start(), calls=%async_computation.11 | async-start | bytes 3244032 | tf_op jit(solution)/shard_map/reduce_scatter | solution.py:93
  214.7 1.0 copy-start.15
  219.6 12.2 %copy-start.16 = (s32[192,6]{0,1:T(8,128)S(1)}, s32[192,6]{0,1:T(8,128)}, u32[]{:S(2)}) copy-start(s32[192,6]{0,1:T(8,128)} %param.8) | copy-start | bytes 13828
  226.0 18.8 %all-to-all-start.1 = ((bf16[8,32,2048]{2,1,0:T(8,128)(2,1)}), bf16[8,32,2048]{2,1,0:T(8,128)(2,1)S(1)}, u32[]{:S(2)}, u32[]{:S(2)}) async-start(bf16[8,32,2048]{2,1,0:T(8,128)(2,1)} %bitcast.107), calls=%async_computation.1 | async-start | bytes 2097152 | tf_op jit(solution)/shard_map/all_to_all | solution.py:71
  265.2 2.1 copy-start.9
  267.3 4.1 copy-start.5
  267.3 4.1 copy-start.6
  267.3 4.1 copy-start.7
  267.3 4.1 copy-start.8
  267.3 4.1 copy-start.10
  267.3 4.1 copy-start.11
  (3 other events, 2.7 us)
Sparse Core Ops, SparseCore 0:
  10.6 64.9 all-gather.7
  78.1 54.3 all-gather.5
  135.1 54.8 all-gather.3
  197.8 93.4 reduce-scatter.7
  295.6 93.0 reduce-scatter.3
  392.5 93.1 reduce-scatter.5
where the time goes:
time: 495 us; the launch traced here: 494 us
  waiting for transfers between devices  374 us (76%)
  local copies, waits for them, and re-layouts  33.9 us (7%)
  matrix products  29.4 us (6%)
  starting transfers between devices  23.5 us (5%)
  other arithmetic  19.1 us (4%)
  between operations  14.4 us (3%)
    reduce_scatter x1, waiting for transfers between devices, shards(): lax.psum_scatter(term_gate.astype(jnp.bfloat16), 'dp', scatter_dimension=...  95.8 us
    reduce_scatter x1, waiting for transfers between devices, shards(): lax.psum_scatter(term_up.astype(jnp.bfloat16), 'dp', scatter_dimension=0,...  95.4 us
    all_gather x1, waiting for transfers between devices, shards(): lax.all_gather(w_gate, 'dp', axis=1, tiled=True)  53.7 us
    all_gather x1, waiting for transfers between devices, shards(): lax.all_gather(w_up, 'dp', axis=1, tiled=True)  52.9 us
    all_gather x1, waiting for transfers between devices, shards(): lax.all_gather(w_down, 'dp', axis=1, tiled=True)  27.3 us
    reduce_scatter x1, waiting for transfers between devices, shards(): lax.psum_scatter(term_down.astype(jnp.bfloat16), 'dp', scatter_dimension=...  18 us
    gather x6, local copies, waits for them, and re-layouts, shards(): back_out[rows_pick].astype(jnp.float32)  12.3 us
    gather x6, local copies, waits for them, and re-layouts, shards(): back_in[rows_pick].astype(jnp.float32)  12.2 us
  transfers between devices with their start and end apart: 10, of which 9 were waited for; matrix products, arithmetic and copies ran while one was open for 14% of the time, Pallas kernels for 0%

commit v1 on v0

--- a/solution.py
+++ b/solution.py
@@ -2,6 +2,7 @@
 import jax.numpy as jnp
 from jax import lax
 from jax.sharding import PartitionSpec as P
+from jax.lax import all_to_all, axis_size
 
 CAP = 32
 
@@ -39,7 +40,9 @@
     full_gate, full_up, full_down = (
         lax.all_gather(w_gate, "dp", axis=1, tiled=True),
         lax.all_gather(w_up, "dp", axis=1, tiled=True),
-        lax.all_gather(w_down, "dp", axis=1, tiled=True),
+        jnp.concatenate(
+            all_to_all(jnp.stack([w_down for _ in range(axis_size("dp"))]), "dp", 0, 0), 1
+        ),
     )
     recv_x, recv_d = (
         lax.all_to_all(send_x, "expert", split_axis=0, concat_axis=0, tiled=True),

time: 495 us -> 478 us (0.966)
  waiting for transfers between devices: 374 us -> 331 us
  blocking collectives: 0 us -> 22.1 us
  starting transfers between devices: 23.5 us -> 28.7 us
    reduce_scatter x1, waiting for transfers between devices: 18 us -> 95.3 us  [shards(): lax.psum_scatter(term_down.astype(jnp.bfloat16), 'dp', scatter_dimension=...]
    reduce_scatter x1, waiting for transfers between devices: 95.4 us -> 20.4 us  [shards(): lax.psum_scatter(term_up.astype(jnp.bfloat16), 'dp', scatter_dimension=0,...]
    all_to_all x1, waiting for transfers between devices: 11.4 us -> 81.2 us  [shards(): all_to_all(jnp.stack([w_down for _ in range(axis_size('dp'))]), 'dp', 0, 0)]
    all_gather x1, waiting for transfers between devices: 52.9 us -> 0.01 us  [shards(): lax.all_gather(w_up, 'dp', axis=1, tiled=True)]
    all_gather x1, waiting for transfers between devices: 53.7 us -> 1.97 us  [shards(): lax.all_gather(w_gate, 'dp', axis=1, tiled=True)]
    all_gather x1 -> x0, waiting for transfers between devices: 27.3 us -> none  [shards(): lax.all_gather(w_down, 'dp', axis=1, tiled=True)]
    all_to_all x0 -> x1, blocking collectives: none -> 22.1 us  [shards(): lax.all_to_all(send_d, 'expert', split_axis=0, concat_axis=0, tiled=True)]
    all_to_all x1, waiting for transfers between devices: 0.01 us -> 19.2 us  [shards(): lax.all_to_all(send_x, 'expert', split_axis=0, concat_axis=0, tiled=True)]
  transfers between devices with their start and end apart: 10 -> 9, of which waited for: 9 -> 8; matrix products, arithmetic and copies ran while one was open for 14% -> 15% of each run, Pallas kernels for 0% -> 0%
where the time goes in v1:
time: 478 us; the launch traced here: 477 us
  waiting for transfers between devices  331 us (69%)
  local copies, waits for them, and re-layouts  34 us (7%)
  matrix products  29.1 us (6%)
  starting transfers between devices  28.7 us (6%)
  blocking collectives  22.1 us (5%)
  other arithmetic  17.9 us (4%)
  between operations  14.1 us (3%)
    reduce_scatter x1, waiting for transfers between devices, shards(): lax.psum_scatter(term_gate.astype(jnp.bfloat16), 'dp', scatter_dimension=...  95.9 us
    reduce_scatter x1, waiting for transfers between devices, shards(): lax.psum_scatter(term_down.astype(jnp.bfloat16), 'dp', scatter_dimension=...  95.3 us
    all_to_all x1, waiting for transfers between devices, shards(): all_to_all(jnp.stack([w_down for _ in range(axis_size('dp'))]), 'dp', 0, 0)  81.2 us
    all_to_all x1, blocking collectives, shards(): lax.all_to_all(send_d, 'expert', split_axis=0, concat_axis=0, tiled=True)  22.1 us
    reduce_scatter x1, waiting for transfers between devices, shards(): lax.psum_scatter(term_up.astype(jnp.bfloat16), 'dp', scatter_dimension=0,...  20.4 us
    all_to_all x1, waiting for transfers between devices, shards(): lax.all_to_all(send_x, 'expert', split_axis=0, concat_axis=0, tiled=True)  19.2 us
    gather x6, local copies, waits for them, and re-layouts, shards(): back_in[rows_pick].astype(jnp.float32)  12.3 us
    gather x6, local copies, waits for them, and re-layouts, shards(): back_out[rows_pick].astype(jnp.float32)  12.2 us
  transfers between devices with their start and end apart: 9, of which 8 were waited for; matrix products, arithmetic and copies ran while one was open for 15% of the time, Pallas kernels for 0%

profile of v1, /device:TPU:2, one launch (start us, length us, event | category | flops | bytes accessed | tf_op | source)
XLA Modules:
  0.0 477.4 jit_solution(9331348633105131189)
XLA Ops:
  10.3 2.3 reduce-window.6
  16.2 22.1 %all_to_all.25 = bf16[8,32,2048]{2,1,0:T(8,128)(2,1)S(1)} all-to-all(bf16[8,32,2048]{2,1,0:T(8,128)(2,1)S(1)} %fusion.15), channel_id=1, replica_groups=mesh['dp'=32,'expert'=8] {'expert'}, dimensions={0} | all-to-all | bytes 2097152 | tf_op jit(solution)/shard_map/all_to_all | solution.py:49
  40.3 11.9 %all-to-all-start.1 = ((bf16[32,1,64,768]{3,2,1,0:T(8,128)(2,1)}), bf16[32,1,64,768]{3,2,1,0:T(8,128)(2,1)}, u32[]{:S(2)}, u32[]{:S(2)}) async-start(bf16[32,1,64,768]{3,2,1,0:T(8,128)(2,1)} %stack.2), calls=%async_computation.1 | async-start | bytes 6291456 | tf_op jit(solution)/shard_map/all_to_all | solution.py:44
  53.0 2.3 gather_fusion
  55.3 2.3 broadcast_select_fusion
  57.7 81.2 %all-to-all-done.1 = bf16[32,1,64,768]{3,2,1,0:T(8,128)(2,1)} async-done(((bf16[32,1,64,768]{3,2,1,0:T(8,128)(2,1)}), bf16[32,1,64,768]{3,2,1,0:T(8,128)(2,1)}, u32[]{:S(2)}, u32[]{:S(2)}) %all-to-all-start.1) | async-done | bytes 3145760 | tf_op jit(solution)/shard_map/all_to_all | solution.py:44
  138.8 5.8 %all-to-all-start = ((bf16[8,32,2048]{2,1,0:T(8,128)(2,1)}), bf16[8,32,2048]{2,1,0:T(8,128)(2,1)S(1)}, u32[]{:S(2)}, u32[]{:S(2)}) async-start(bf16[8,32,2048]{2,1,0:T(8,128)(2,1)} %broadcast_select_fusion), calls=%async_computation | async-start | bytes 2097152 | tf_op jit(solution)/shard_map/all_to_all | solution.py:48
  144.7 3.7 fusion.28
  148.4 19.2 %all-to-all-done = bf16[8,32,2048]{2,1,0:T(8,128)(2,1)S(1)} async-done(((bf16[8,32,2048]{2,1,0:T(8,128)(2,1)}), bf16[8,32,2048]{2,1,0:T(8,128)(2,1)S(1)}, u32[]{:S(2)}, u32[]{:S(2)}) %all-to-all-start) | async-done | bytes 1048608 | tf_op jit(solution)/shard_map/all_to_all | solution.py:48
  167.6 3.8 fusion.2
  173.4 4.3 multiply_convert_fusion.1
  178.5 2.7 convolution_convert_fusion.1
  181.3 2.7 convolution_convert_fusion.2
  185.0 3.0 fusion
  190.1 5.3 %all-to-all-start.4 = ((bf16[8,32,2048]{2,1,0:T(8,128)(2,1)}), bf16[8,32,2048]{2,1,0:T(8,128)(2,1)S(1)}, u32[]{:S(2)}, u32[]{:S(2)}) async-start(bf16[8,32,2048]{2,1,0:T(8,128)(2,1)} %bitcast.101), calls=%async_computation.4 | async-start | bytes 2097152 | tf_op jit(solution)/shard_map/all_to_all | solution.py:81
  195.4 2.8 convolution_convert_fusion
  198.2 3.9 convolution_convert_fusion.3
  202.2 7.3 %all-to-all-done.4 = bf16[8,32,2048]{2,1,0:T(8,128)(2,1)S(1)} async-done(((bf16[8,32,2048]{2,1,0:T(8,128)(2,1)}), bf16[8,32,2048]{2,1,0:T(8,128)(2,1)S(1)}, u32[]{:S(2)}, u32[]{:S(2)}) %all-to-all-start.4) | async-done | bytes 1048608 | tf_op jit(solution)/shard_map/all_to_all | solution.py:81
  209.5 5.6 %all-to-all-start.2 = ((bf16[8,32,2048]{2,1,0:T(8,128)(2,1)}), bf16[8,32,2048]{2,1,0:T(8,128)(2,1)S(1)}, u32[]{:S(2)}, u32[]{:S(2)}) async-start(bf16[8,32,2048]{2,1,0:T(8,128)(2,1)} %bitcast.104), calls=%async_computation.2 | async-start | bytes 2097152 | tf_op jit(solution)/shard_map/all_to_all | solution.py:74
  219.6 8.7 %all-to-all-done.2 = bf16[8,32,2048]{2,1,0:T(8,128)(2,1)S(1)} async-done(((bf16[8,32,2048]{2,1,0:T(8,128)(2,1)}), bf16[8,32,2048]{2,1,0:T(8,128)(2,1)S(1)}, u32[]{:S(2)}, u32[]{:S(2)}) %all-to-all-start.2) | async-done | bytes 1048608 | tf_op jit(solution)/shard_map/all_to_all | solution.py:74
  248.7 3.9 add_convert_fusion
  254.5 20.4 %reduce-scatter.6.cloned.1.call-done = bf16[64,768]{1,0:T(8,128)(2,1)} async-done(((bf16[2048,768]{1,0:T(8,128)(2,1)}), bf16[64,768]{1,0:T(8,128)(2,1)}) %reduce-scatter.6.cloned.1.call-update) | async-done | bytes 98320 | tf_op jit(solution)/shard_map/reduce_scatter | solution.py:96
  276.5 95.9 %reduce-scatter.4.cloned.1.call-done = bf16[64,768]{1,0:T(8,128)(2,1)} async-done(((bf16[2048,768]{1,0:T(8,128)(2,1)}), bf16[64,768]{1,0:T(8,128)(2,1)}) %reduce-scatter.4.cloned.1.call-update) | async-done | bytes 98320 | tf_op jit(solution)/shard_map/reduce_scatter | solution.py:93
  374.0 95.3 %reduce-scatter.8.cloned.1.call-done = bf16[64,768]{1,0:T(8,128)(2,1)} async-done(((bf16[2048,768]{1,0:T(8,128)(2,1)}), bf16[64,768]{1,0:T(8,128)(2,1)}) %reduce-scatter.8.cloned.1.call-update) | async-done | bytes 98320 | tf_op jit(solution)/shard_map/reduce_scatter | solution.py:99
  (98 shorter events, 46.6 us)
Async XLA Ops:
  7.2 7.3 %copy-start = (bf16[192,2048]{1,0:T(8,128)(2,1)S(1)}, bf16[192,2048]{1,0:T(8,128)(2,1)}, u32[]{:S(2)}) copy-start(bf16[192,2048]{1,0:T(8,128)(2,1)} %param.13) | copy-start | bytes 2359300
  7.2 160.5 %all-gather.5.cloned.1.call-start = ((), (), s32[]{:S(2)}) async-start(), calls=%async_computation.9 | async-start | bytes 3244032 | tf_op jit(solution)/shard_map/all_gather | solution.py:42
  16.2 22.2 %copy-start.14 = (bf16[1,64,768]{2,1,0:T(8,128)(2,1)S(1)}, bf16[1,64,768]{2,1,0:T(8,128)(2,1)}, u32[]{:S(2)}) copy-start(bf16[1,64,768]{2,1,0:T(8,128)(2,1)} %param.12) | copy-start | bytes 294916
  40.3 12.7 %copy-start.1 = (bf16[192,2048]{1,0:T(8,128)(2,1)S(1)}, bf16[192,2048]{1,0:T(8,128)(2,1)}, u32[]{:S(2)}) copy-start(bf16[192,2048]{1,0:T(8,128)(2,1)} %param.7) | copy-start | bytes 2359300
  40.3 98.5 %all-to-all-start.1 = ((bf16[32,1,64,768]{3,2,1,0:T(8,128)(2,1)}), bf16[32,1,64,768]{3,2,1,0:T(8,128)(2,1)}, u32[]{:S(2)}, u32[]{:S(2)}) async-start(bf16[32,1,64,768]{3,2,1,0:T(8,128)(2,1)} %stack.2), calls=%async_computation.1 | async-start | bytes 6291456 | tf_op jit(solution)/shard_map/all_to_all | solution.py:44
  52.2 121.2 %all-gather.3.cloned.1.call-start = ((), (), s32[]{:S(2)}) async-start(), calls=%async_computation.8 | async-start | bytes 3244032 | tf_op jit(solution)/shard_map/all_gather | solution.py:41
  138.8 28.8 %all-to-all-start = ((bf16[8,32,2048]{2,1,0:T(8,128)(2,1)}), bf16[8,32,2048]{2,1,0:T(8,128)(2,1)S(1)}, u32[]{:S(2)}, u32[]{:S(2)}) async-start(bf16[8,32,2048]{2,1,0:T(8,128)(2,1)} %broadcast_select_fusion), calls=%async_computation | async-start | bytes 2097152 | tf_op jit(solution)/shard_map/all_to_all | solution.py:48
  144.7 130.2 %reduce-scatter.6.cloned.1.call-start = ((), (), s32[]{:S(2)}) async-start(), calls=%async_computation.11 | async-start | bytes 3244032 | tf_op jit(solution)/shard_map/reduce_scatter | solution.py:96
  181.2 191.2 %reduce-scatter.4.cloned.1.call-start = ((), (), s32[]{:S(2)}) async-start(), calls=%async_computation.10 | async-start | bytes 3244032 | tf_op jit(solution)/shard_map/reduce_scatter | solution.py:93
  184.0 1.0 copy-start.12
  185.0 3.1 copy-start.2
  190.1 5.3 %copy-start.13 = (bf16[256,768]{1,0:T(8,128)(2,1)S(1)}, bf16[256,768]{1,0:T(8,128)(2,1)}, u32[]{:S(2)}) copy-start(bf16[256,768]{1,0:T(8,128)(2,1)} %get-tuple-element.16) | copy-start | bytes 1179652
  190.1 19.4 %all-to-all-start.4 = ((bf16[8,32,2048]{2,1,0:T(8,128)(2,1)}), bf16[8,32,2048]{2,1,0:T(8,128)(2,1)S(1)}, u32[]{:S(2)}, u32[]{:S(2)}) async-start(bf16[8,32,2048]{2,1,0:T(8,128)(2,1)} %bitcast.101), calls=%async_computation.4 | async-start | bytes 2097152 | tf_op jit(solution)/shard_map/all_to_all | solution.py:81
  195.4 273.9 %reduce-scatter.8.cloned.1.call-start = ((), (), s32[]{:S(2)}) async-start(), calls=%async_computation.12 | async-start | bytes 3244032 | tf_op jit(solution)/shard_map/reduce_scatter | solution.py:99
  202.2 13.1 %copy-start.15 = (s32[192,6]{0,1:T(8,128)S(1)}, s32[192,6]{0,1:T(8,128)}, u32[]{:S(2)}) copy-start(s32[192,6]{0,1:T(8,128)} %param.8) | copy-start | bytes 13828
  209.5 18.8 %all-to-all-start.2 = ((bf16[8,32,2048]{2,1,0:T(8,128)(2,1)}), bf16[8,32,2048]{2,1,0:T(8,128)(2,1)S(1)}, u32[]{:S(2)}, u32[]{:S(2)}) async-start(bf16[8,32,2048]{2,1,0:T(8,128)(2,1)} %bitcast.104), calls=%async_computation.2 | async-start | bytes 2097152 | tf_op jit(solution)/shard_map/all_to_all | solution.py:74
  246.6 2.0 copy-start.7
  246.6 2.0 copy-start.8
  248.6 4.0 copy-start.3
  248.6 4.0 copy-start.4
  248.6 4.0 copy-start.5
  248.6 4.0 copy-start.6
  248.7 4.0 copy-start.9
  248.7 4.0 copy-start.10
  (1 other events, 0.7 us)
Sparse Core Ops, SparseCore 0:
  10.6 75.0 all-gather.4
  88.1 85.2 all-gather.2
  181.3 93.5 reduce-scatter.5
  279.2 93.1 reduce-scatter.3
  376.1 93.1 reduce-scatter.7
